TPU v7x, 32 devices: a whole 2x2x4 slice. The times are simulated.
32 devices in a mesh: rep: 4 (over y, x), exp: 8 (over z, core).
Axes of the slice: x: 2, y: 2, z: 4, core: 2. Of those that a mesh axis runs over, the one named last changes fastest.
Arguments:
- tokens: bfloat16 [4096, 3584], P(('rep', 'exp')), may hold values from -6 to 6
- routes: int32 [4096, 8], P(('rep', 'exp')), may hold values from 0 to 255, as said below
- gates: float32 [4096, 8], P(('rep', 'exp')), may hold values from 0.1 to 1
- gate_weight: bfloat16 [8, 3584, 2048], P('exp', None, 'rep'), may hold values from -0.09375 to 0.09375
- up_weight: bfloat16 [8, 3584, 2048], P('exp', None, 'rep'), may hold values from -0.09375 to 0.09375
- down_weight: bfloat16 [8, 2048, 3584], P('exp', 'rep'), may hold values from -0.125 to 0.125
- grad_out: bfloat16 [4096, 3584], P(('rep', 'exp')), may hold values from -6 to 6
Outputs:
- combined: bfloat16 [4096, 3584], P(('rep', 'exp'))
- token_grad: bfloat16 [4096, 3584], P(('rep', 'exp'))
- gate_weight_grad: bfloat16 [8, 3584, 2048], P('exp', None, 'rep')
- up_weight_grad: bfloat16 [8, 3584, 2048], P('exp', None, 'rep')
- down_weight_grad: bfloat16 [8, 2048, 3584], P('exp', 'rep')
Inputs may be any that keep to these rules, and one draw needn't show every extreme that they name: `routes`: each row names 8 different experts and at most one of experts 0 to 7. In the rows of one device (aligned blocks of 128 rows) each of experts 0 to 7 is named by at most 2 rows, and one of them, the same in every block, by exactly 2 rows.
All inputs are finite; a program needn't handle non-finite values.
Results may differ from a plain program's by a relative error of at most 0.012.
Values may be sent and summed in bfloat16 or wider, within the bound.
A program may use at most 128 MiB of HBM per device.

v0:
```python
import jax
import jax.numpy as jnp
from jax import lax
from jax.sharding import PartitionSpec as P

CAP = 2


def deliver(slot_rows):
    landed = lax.all_to_all(slot_rows, "exp", split_axis=0, concat_axis=0, tiled=True)
    arrived = lax.all_gather(landed, "rep", axis=1, tiled=True)
    return arrived.reshape(-1, arrived.shape[-1])


def reduce_rows(term_fn, row_count):
    return lax.psum_scatter(
        term_fn(jnp.int32(0), row_count * lax.axis_size("rep")).astype(jnp.bfloat16),
        "rep",
        scatter_dimension=0,
        tiled=True,
    ).astype(jnp.float32)


def send_back(slot_rows):
    return lax.all_to_all(slot_rows, "exp", split_axis=0, concat_axis=0, tiled=True)


def on_device(tokens, routes, gates, gate_weight, up_weight, down_weight, grad_out):
    features = tokens.shape[1]
    experts_here = lax.axis_size("exp")
    groups = lax.axis_size("rep")
    slot_total = experts_here * CAP
    owners = jnp.arange(experts_here, dtype=jnp.int32)
    matches = routes[:, :, None] == owners[None, None, :]
    picked = jnp.any(matches, axis=1).astype(jnp.int32)
    weights_sel = jnp.sum(jnp.where(matches, gates[:, :, None], 0.0), axis=1)
    before = jnp.cumsum(picked, axis=0) - picked
    picked_wide = jnp.repeat(picked, CAP, axis=1)
    before_wide = jnp.repeat(before, CAP, axis=1)
    position = jnp.arange(slot_total, dtype=jnp.int32) % CAP
    placing = (picked_wide == 1) & (before_wide == position[None, :])
    placing_bf = placing.astype(jnp.bfloat16)
    combine_weights = jnp.where(placing, jnp.repeat(weights_sel, CAP, axis=1), 0.0)
    slot_gate = jnp.sum(combine_weights, axis=0)
    first_dims = (((0,), (0,)), ((), ()))
    send_rows = lax.dot_general(placing_bf, tokens, first_dims, preferred_element_type=jnp.float32)
    send_rows = send_rows.astype(jnp.bfloat16).reshape(experts_here, CAP, features)
    grad_rows = lax.dot_general(
        placing_bf, grad_out, first_dims, preferred_element_type=jnp.float32
    )
    send_grads = (
        (slot_gate[:, None] * grad_rows).astype(jnp.bfloat16).reshape(experts_here, CAP, features)
    )
    rows_all = deliver(send_rows)
    units = gate_weight.shape[2]
    joined = jnp.concatenate([gate_weight[0], up_weight[0]], axis=1)
    projected = jnp.dot(rows_all, joined, preferred_element_type=jnp.float32)
    gate_pre = projected[:, :units]
    up_pre = projected[:, units:]
    sigmoid_gate = jax.nn.sigmoid(gate_pre)
    active = gate_pre * sigmoid_gate
    hidden = (active * up_pre).astype(jnp.bfloat16)

    def down_term(offset, amount):
        grid = hidden.reshape(experts_here, groups, CAP, units)
        term = jnp.einsum("sgcu,ud->gscd", grid, down_weight[0], preferred_element_type=jnp.float32)
        return term.reshape(-1, features)

    mine_out = reduce_rows(down_term, slot_total).astype(jnp.bfloat16)
    returned = send_back(mine_out.reshape(experts_here, CAP, features)).reshape(
        slot_total, features
    )
    combined = jnp.dot(
        combine_weights, returned.astype(jnp.float32), precision=lax.Precision.HIGHEST
    ).astype(jnp.bfloat16)
    grads_all = deliver(send_grads)
    last_dims = (((1,), (1,)), ((), ()))
    hidden_grad = lax.dot_general(
        grads_all, down_weight[0], last_dims, preferred_element_type=jnp.float32
    )
    gate_grad = hidden_grad * up_pre * sigmoid_gate * (1.0 + gate_pre * (1.0 - sigmoid_gate))
    up_grad = hidden_grad * active
    both_grad = jnp.concatenate([gate_grad, up_grad], axis=1).astype(jnp.bfloat16)
    down_weight_grad = lax.dot_general(
        hidden, grads_all, first_dims, preferred_element_type=jnp.float32
    ).astype(jnp.bfloat16)[None]
    joined_grad = lax.dot_general(
        rows_all, both_grad, first_dims, preferred_element_type=jnp.float32
    )
    gate_weight_grad = joined_grad[:, :units].astype(jnp.bfloat16)[None]
    up_weight_grad = joined_grad[:, units:].astype(jnp.bfloat16)[None]

    def input_term(offset, amount):
        grid = both_grad.reshape(experts_here, groups, CAP, 2 * units)
        term = jnp.einsum("sgcu,du->gscd", grid, joined, preferred_element_type=jnp.float32)
        return term.reshape(-1, features)

    mine_grad = reduce_rows(input_term, slot_total).astype(jnp.bfloat16)
    returned_grad = send_back(mine_grad.reshape(experts_here, CAP, features)).reshape(
        slot_total, features
    )
    token_grad = jnp.dot(placing_bf, returned_grad, preferred_element_type=jnp.float32).astype(
        jnp.bfloat16
    )
    return (combined, token_grad, gate_weight_grad, up_weight_grad, down_weight_grad)


def solution(mesh):
    placed = (
        P(("rep", "exp"), None),
        P(("rep", "exp"), None),
        P(("rep", "exp"), None),
        P("exp", None, "rep"),
        P("exp", None, "rep"),
        P("exp", "rep", None),
        P(("rep", "exp"), None),
    )
    return jax.shard_map(
        on_device,
        mesh=mesh,
        in_specs=placed,
        out_specs=(
            P(("rep", "exp"), None),
            P(("rep", "exp"), None),
            P("exp", None, "rep"),
            P("exp", None, "rep"),
            P("exp", "rep", None),
        ),
        check_vma=False,
    )
```

profile of v0, /device:TPU:0, one launch (start us, length us, event | category | flops | bytes accessed | tf_op | source)
XLA Modules:
  0.0 134.1 jit_solution(3095305914191506199)
XLA Ops:
  7.2 0.8 fusion.35
  8.1 0.2 reduce_window_sum.11
  8.4 0.7 select_reduce_fusion
  9.5 0.2 fusion.13
  9.8 0.7 reshape.86
  10.5 6.4 %all-to-all-start.2 = ((bf16[8,2,3584]{2,1,0:T(2,128)(2,1)}), bf16[8,2,3584]{2,1,0:T(2,128)(2,1)S(1)}, u32[]{:S(2)}, u32[]{:S(2)}) async-start(bf16[8,2,3584]{2,1,0:T(2,128)(2,1)} %reshape.86), calls=%async_computation.3 | async-start | bytes 229376 | tf_op jit(solution)/shard_map/all_to_all | solution.py:10
  16.8 1.4 %convolution_convert_fusion.3 = bf16[16,3584]{1,0:T(8,128)(2,1)S(1)} fusion(pred[128,16]{0,1:T(8,128)(4,1)S(1)} %compare_and_fusion.1, bf16[128,3584]{1,0:T(8,128)(2,1)} %param.7), kind=kOutput, calls=%fused_computation.17 | convolution fusion | flops 14737408 | bytes 1034240 | tf_op jit(solution)/shard_map/dot_general | solution.py:46
  18.2 0.7 reshape.82
  18.9 4.4 %all-to-all-done.2 = bf16[8,2,3584]{2,1,0:T(2,128)(2,1)S(1)} async-done(((bf16[8,2,3584]{2,1,0:T(2,128)(2,1)}), bf16[8,2,3584]{2,1,0:T(2,128)(2,1)S(1)}, u32[]{:S(2)}, u32[]{:S(2)}) %all-to-all-start.2) | async-done | bytes 114720 | tf_op jit(solution)/shard_map/all_to_all | solution.py:10
  23.4 3.4 %all-to-all-start = ((bf16[8,2,3584]{2,1,0:T(2,128)(2,1)}), bf16[8,2,3584]{2,1,0:T(2,128)(2,1)S(1)}, u32[]{:S(2)}, u32[]{:S(2)}) async-start(bf16[8,2,3584]{2,1,0:T(2,128)(2,1)} %reshape.82), calls=%async_computation | async-start | bytes 229376 | tf_op jit(solution)/shard_map/all_to_all | solution.py:10
  26.8 9.8 %all_gather.7 = bf16[8,8,3584]{2,0,1:T(8,128)(2,1)S(1)} all-gather(bf16[8,2,3584]{2,0,1:T(8,128)(2,1)S(1)} %copy.90), channel_id=1, replica_groups=mesh['rep'=4,'exp'=8] {'rep'}, dimensions={1}, use_global_device_ids=true | all-gather | bytes 573440 | tf_op jit(solution)/shard_map/all_gather | solution.py:11
  36.6 10.4 %all_gather.6 = bf16[8,8,3584]{2,0,1:T(8,128)(2,1)S(1)} all-gather(bf16[8,2,3584]{2,0,1:T(8,128)(2,1)S(1)} %copy.84), channel_id=1, replica_groups=mesh['rep'=4,'exp'=8] {'rep'}, dimensions={1}, use_global_device_ids=true | all-gather | bytes 573440 | tf_op jit(solution)/shard_map/all_gather | solution.py:11
  47.0 4.1 %fusion.5 = f32[64,1024]{1,0:T(8,128)S(1)} fusion(bf16[3584,512]{1,0:T(8,128)(2,1)} %bitcast.61, bf16[3584,512]{1,0:T(8,128)(2,1)} %bitcast.63, bf16[8,8,3584]{2,0,1:T(8,128)(2,1)S(1)} %all_gather.6), kind=kOutput, calls=%fused_computation.10 | convolution fusion | flops 484442112 | bytes 8060928 | tf_op jit(solution)/shard_map/dot_general | solution.py:57
  51.2 1.2 multiply_convert_fusion.1
  52.6 5.5 %fusion.9 = bf16[4,8,2,3584]{3,1,2,0:T(8,128)(2,1)S(1)} fusion(bf16[3584,512]{1,0:T(8,128)(2,1)} %bitcast.62, bf16[3584,512]{1,0:T(8,128)(2,1)} %bitcast.64, bf16[8,4,2,512]{3,0,2,1:T(8,128)(2,1)S(1)} %copy.93, bf16[8,4,2,512]{3,0,2,1:T(8,128)(2,1)S(1)} %copy.92), kind=kOutput, calls=%fused_computation.13 | convolution fusion | flops 484933632 | bytes 7929856 | tf_op jit(solution)/shard_map/sgcu,du->gscd/dot_general | solution.py:95
  58.1 0.4 copy.94
  58.5 0.9 convert_element_type.59
  59.5 2.8 %fusion.12 = bf16[4,8,2,3584]{3,1,2,0:T(8,128)(2,1)S(1)} fusion(bf16[1,512,3584]{2,1,0:T(8,128)(2,1)} %param.12, bf16[8,4,2,512]{3,2,1,0:T(2,128)(2,1)S(1)} %reshape.84), kind=kOutput, calls=%fused_computation.14 | convolution fusion | flops 235110400 | bytes 4194304 | tf_op jit(solution)/shard_map/sgcu,ud->gscd/dot_general | solution.py:66
  62.3 0.4 copy.87
  62.7 0.9 convert_element_type.54
  63.6 5.1 %convolution_convert_fusion = bf16[3584,1024]{1,0:T(8,128)(2,1)} fusion(bf16[8,8,3584]{2,0,1:T(8,128)(2,1)S(1)} %all_gather.6, bf16[64,512]{1,0:T(8,128)(2,1)S(1)} %get-tuple-element.10, bf16[64,512]{1,0:T(8,128)(2,1)S(1)} %get-tuple-element.9), kind=kOutput, calls=%fused_computation | convolution fusion | flops 473694208 | bytes 7929856 | tf_op jit(solution)/shard_map/dot_general | solution.py:87
  68.7 15.7 %reduce-scatter.5.cloned.1.call-done = bf16[16,3584]{1,0:T(8,128)(2,1)} async-done(((bf16[64,3584]{1,0:T(8,128)(2,1)}), bf16[16,3584]{1,0:T(8,128)(2,1)}) %reduce-scatter.5.cloned.1.call-update) | async-done | bytes 114704 | tf_op jit(solution)/shard_map/reduce_scatter | solution.py:16
  84.4 1.6 %reshape.88 = bf16[8,2,3584]{2,1,0:T(2,128)(2,1)} reshape(bf16[16,3584]{1,0:T(8,128)(2,1)} %reduce-scatter.5.cloned.1.call-done) | data formatting | bytes 229376 | tf_op jit(solution)/shard_map/reshape | solution.py:99
  86.0 4.6 %all-to-all-start.3 = ((bf16[8,2,3584]{2,1,0:T(2,128)(2,1)}), bf16[8,2,3584]{2,1,0:T(2,128)(2,1)S(1)}, u32[]{:S(2)}, u32[]{:S(2)}) async-start(bf16[8,2,3584]{2,1,0:T(2,128)(2,1)} %reshape.88), calls=%async_computation.5 | async-start | bytes 229376 | tf_op jit(solution)/shard_map/all_to_all | solution.py:25
  90.5 6.7 %slice_bitcast_fusion = (bf16[1,3584,512]{2,1,0:T(8,128)(2,1)}, bf16[1,3584,512]{2,1,0:T(8,128)(2,1)}) fusion(bf16[3584,1024]{1,0:T(8,128)(2,1)} %convolution_convert_fusion), kind=kLoop, calls=%fused_computation.18 | loop fusion | bytes 14680064 | tf_op jit(solution)/shard_map/broadcast_in_dim | solution.py:91
  97.2 3.0 %fusion.2 = bf16[1,512,3584]{2,1,0:T(8,128)(2,1)} fusion(bf16[64,512]{1,0:T(8,128)(2,1)S(1)} %get-tuple-element.11, bf16[8,8,3584]{2,0,1:T(8,128)(2,1)S(1)} %all_gather.7), kind=kOutput, calls=%fused_computation.5 | convolution fusion | flops 236716032 | bytes 4194304 | tf_op jit(solution)/shard_map/dot_general | solution.py:84
  100.2 12.5 %reduce-scatter.3.cloned.1.call-done = bf16[16,3584]{1,0:T(8,128)(2,1)} async-done(((bf16[64,3584]{1,0:T(8,128)(2,1)}), bf16[16,3584]{1,0:T(8,128)(2,1)}) %reduce-scatter.3.cloned.1.call-update) | async-done | bytes 114704 | tf_op jit(solution)/shard_map/reduce_scatter | solution.py:16
  112.7 1.6 %reshape.85 = bf16[8,2,3584]{2,1,0:T(2,128)(2,1)} reshape(bf16[16,3584]{1,0:T(8,128)(2,1)} %reduce-scatter.3.cloned.1.call-done) | data formatting | bytes 229376 | tf_op jit(solution)/shard_map/reshape | solution.py:70
  114.3 4.6 %all-to-all-start.1 = ((bf16[8,2,3584]{2,1,0:T(2,128)(2,1)}), bf16[8,2,3584]{2,1,0:T(2,128)(2,1)S(1)}, u32[]{:S(2)}, u32[]{:S(2)}) async-start(bf16[8,2,3584]{2,1,0:T(2,128)(2,1)} %reshape.85), calls=%async_computation.2 | async-start | bytes 229376 | tf_op jit(solution)/shard_map/all_to_all | solution.py:25
  118.9 1.4 %fusion.4 = bf16[128,3584]{1,0:T(8,128)(2,1)} fusion(bf16[8,2,3584]{2,1,0:T(2,128)(2,1)S(1)} %all-to-all-done.3, pred[128,8,2]{0,2,1:T(4,128)(4,1)S(1)} %get-tuple-element.6), kind=kOutput, calls=%fused_computation.9 | convolution fusion | flops 15138816 | bytes 1034240 | tf_op jit(solution)/shard_map/dot_general | solution.py:102
  120.2 5.2 %all-to-all-done.1 = bf16[8,2,3584]{2,1,0:T(2,128)(2,1)S(1)} async-done(((bf16[8,2,3584]{2,1,0:T(2,128)(2,1)}), bf16[8,2,3584]{2,1,0:T(2,128)(2,1)S(1)}, u32[]{:S(2)}, u32[]{:S(2)}) %all-to-all-start.1) | async-done | bytes 114720 | tf_op jit(solution)/shard_map/all_to_all | solution.py:25
  125.4 1.8 %fusion.3 = bf16[128,3584]{1,0:T(8,128)(2,1)} fusion(bf16[8,2,3584]{2,1,0:T(2,128)(2,1)S(1)} %all-to-all-done.1, f32[128,8,2]{0,2,1:T(2,128)S(1)} %broadcast_select_fusion), kind=kOutput, calls=%fused_computation.8 | convolution fusion | flops 88539136 | bytes 1040384 | tf_op jit(solution)/shard_map/dot_general | solution.py:73
  (31 shorter events, 1.1 us)
Async XLA Ops:
  7.2 2.4 %copy-start = (bf16[128,3584]{1,0:T(8,128)(2,1)S(1)}, bf16[128,3584]{1,0:T(8,128)(2,1)}, u32[]{:S(2)}) copy-start(bf16[128,3584]{1,0:T(8,128)(2,1)} %param.13) | copy-start | bytes 2752516
  10.5 12.9 %all-to-all-start.2 = ((bf16[8,2,3584]{2,1,0:T(2,128)(2,1)}), bf16[8,2,3584]{2,1,0:T(2,128)(2,1)S(1)}, u32[]{:S(2)}, u32[]{:S(2)}) async-start(bf16[8,2,3584]{2,1,0:T(2,128)(2,1)} %reshape.86), calls=%async_computation.3 | async-start | bytes 229376 | tf_op jit(solution)/shard_map/all_to_all | solution.py:10
  23.4 13.2 %all-to-all-start = ((bf16[8,2,3584]{2,1,0:T(2,128)(2,1)}), bf16[8,2,3584]{2,1,0:T(2,128)(2,1)S(1)}, u32[]{:S(2)}, u32[]{:S(2)}) async-start(bf16[8,2,3584]{2,1,0:T(2,128)(2,1)} %reshape.82), calls=%async_computation | async-start | bytes 229376 | tf_op jit(solution)/shard_map/all_to_all | solution.py:10
  26.7 57.6 %reduce-scatter.5.cloned.1.call-start = ((), (), s32[]{:S(2)}) async-start(), calls=%async_computation.7 | async-start | bytes 573440 | tf_op jit(solution)/shard_map/reduce_scatter | solution.py:16
  47.0 4.2 %copy-start.1 = (bf16[1,512,3584]{2,1,0:T(8,128)(2,1)S(1)}, bf16[1,512,3584]{2,1,0:T(8,128)(2,1)}, u32[]{:S(2)}) copy-start(bf16[1,512,3584]{2,1,0:T(8,128)(2,1)} %param.12) | copy-start | bytes 11010052
  59.4 53.3 %reduce-scatter.3.cloned.1.call-start = ((), (), s32[]{:S(2)}) async-start(), calls=%async_computation.6 | async-start | bytes 573440 | tf_op jit(solution)/shard_map/reduce_scatter | solution.py:16
  86.0 28.3 %all-to-all-start.3 = ((bf16[8,2,3584]{2,1,0:T(2,128)(2,1)}), bf16[8,2,3584]{2,1,0:T(2,128)(2,1)S(1)}, u32[]{:S(2)}, u32[]{:S(2)}) async-start(bf16[8,2,3584]{2,1,0:T(2,128)(2,1)} %reshape.88), calls=%async_computation.5 | async-start | bytes 229376 | tf_op jit(solution)/shard_map/all_to_all | solution.py:25
  114.3 11.1 %all-to-all-start.1 = ((bf16[8,2,3584]{2,1,0:T(2,128)(2,1)}), bf16[8,2,3584]{2,1,0:T(2,128)(2,1)S(1)}, u32[]{:S(2)}, u32[]{:S(2)}) async-start(bf16[8,2,3584]{2,1,0:T(2,128)(2,1)} %reshape.85), calls=%async_computation.2 | async-start | bytes 229376 | tf_op jit(solution)/shard_map/all_to_all | solution.py:25
Sparse Core Ops, SparseCore 0:
  59.5 24.7 reduce-scatter.4
  87.7 24.8 reduce-scatter.2
where the time goes:
time: 135 us; the launch traced here: 134 us
  waiting for transfers between devices  37.8 us (28%)
  matrix products  26.5 us (20%)
  blocking collectives  20.2 us (15%)
  starting transfers between devices  19 us (14%)
  local copies, waits for them, and re-layouts  14.5 us (11%)
  between operations  14.2 us (11%)
  other arithmetic  1.97 us (1%)
    reduce_scatter x2, waiting for transfers between devices, reduce_rows(): lax.psum_scatter(term_fn(jnp.int32(0), row_count * lax.axis_size('rep'))....  28.1 us
    all_gather x2, blocking collectives, deliver(): arrived = lax.all_gather(landed, 'rep', axis=1, tiled=True)  20.2 us
    all_to_all x2, starting transfers between devices, deliver(): lax.all_to_all(slot_rows, 'exp', split_axis=0, concat_axis=0, tiled=True)  9.72 us
    all_to_all x2, starting transfers between devices, send_back(): lax.all_to_all(slot_rows, 'exp', split_axis=0, concat_axis=0, tiled=True)  9.18 us
    broadcast_in_dim x1, local copies, waits for them, and re-layouts, on_device(): up_weight_grad = joined_grad[:, units:].astype(jnp.bfloat16)[None]  6.67 us
    dot_general x1, matrix products, input_term(): jnp.einsum('sgcu,du->gscd', grid, joined, preferred_element_type=jnp.floa...  5.49 us
    all_to_all x2, waiting for transfers between devices, send_back(): lax.all_to_all(slot_rows, 'exp', split_axis=0, concat_axis=0, tiled=True)  5.16 us
    dot_general x1, matrix products, on_device(): lax.dot_general(rows_all, both_grad, first_dims, preferred_element_type=j...  5.06 us
  transfers between devices with their start and end apart: 6, of which 4 were waited for; matrix products, arithmetic and copies ran while one was open for 19% of the time, Pallas kernels for 0%

commit v1 on v0

v1 whole, which is shorter than its diff:
```python
import functools

import jax
import jax.numpy as jnp
from jax import lax
from jax.experimental import pallas as pl
from jax.experimental.pallas import tpu as pltpu
from jax.sharding import PartitionSpec as P

CAP = 2
MESH = pl.DeviceIdType.MESH
F32 = jnp.float32
BF16 = jnp.bfloat16
LAST = (((1,), (1,)), ((), ()))
FIRST = (((0,), (0,)), ((), ()))


def exchange_kernel(
    R,
    E,
    routes,
    gates,
    tok_h,
    grad_h,
    wg_h,
    wu_h,
    wd_h,
    rows_o,
    hid_o,
    gg_o,
    ug_o,
    ret_o,
    place_o,
    w_o,
    tg_v,
    wg_v,
    wu_v,
    wd_v,
    sendb,
    land,
    xf,
    part,
    rs,
    back,
    ret,
    in_sem,
    own_sem,
    a2a_s,
    a2a_r,
    ag_s,
    ag_r,
    rs_s,
    rs_r,
    bk_s,
    bk_r,
):
    S = E * CAP
    T, D = tok_h.shape
    U = wg_h.shape[2]
    N = R * S
    me_r = lax.axis_index("rep")
    me_e = lax.axis_index("exp")
    loads = [
        pltpu.make_async_copy(tok_h, tg_v.at[0], in_sem.at[0]),
        pltpu.make_async_copy(grad_h, tg_v.at[1], in_sem.at[1]),
        pltpu.make_async_copy(wg_h.at[0], wg_v, in_sem.at[2]),
        pltpu.make_async_copy(wu_h.at[0], wu_v, in_sem.at[3]),
        pltpu.make_async_copy(wd_h.at[0], wd_v, in_sem.at[4]),
    ]
    for c in loads:
        c.start()
    barrier = pltpu.get_barrier_semaphore()
    for k in range(1, E):
        pl.semaphore_signal(
            barrier, inc=1, device_id=(me_r, lax.rem(me_e + k, E)), device_id_type=MESH
        )
    for j in range(1, R):
        pl.semaphore_signal(
            barrier, inc=1, device_id=(lax.rem(me_r + j, R), me_e), device_id_type=MESH
        )

    live = routes[...] < E
    eid = jnp.sum(jnp.where(live, routes[...].astype(F32) + 1.0, 0.0), axis=1, keepdims=True) - 1.0
    w = jnp.sum(jnp.where(live, gates[...], 0.0), axis=1, keepdims=True)
    lanes = lax.broadcasted_iota(jnp.int32, (T, T), 1)
    subs = lax.broadcasted_iota(jnp.int32, (T, T), 0)
    picked = jnp.where(eid == lanes.astype(F32), 1.0, 0.0)
    lower = jnp.where(lanes < subs, 1.0, 0.0).astype(BF16)
    before = jnp.dot(lower, picked.astype(BF16), preferred_element_type=F32)
    pos = jnp.sum(picked * before, axis=1, keepdims=True)
    slot = jnp.where(eid >= 0.0, eid * CAP + pos, -1.0)
    place_o[...] = jnp.where(slot == lanes[:, :S].astype(F32), 1.0, 0.0).astype(BF16)
    w_o[...] = w
    slot_t = jnp.transpose(jnp.broadcast_to(slot, (T, T)))[:S]
    w_t = jnp.transpose(jnp.broadcast_to(w, (T, T)))[:S]
    placed_t = slot_t == subs[:S].astype(F32)
    place_t = jnp.where(placed_t, 1.0, 0.0).astype(BF16)
    slot_gate = jnp.sum(jnp.where(placed_t, w_t, 0.0), axis=1, keepdims=True)

    pl.semaphore_wait(barrier, E + R - 2)

    def forward(t, src, p):
        for j in range(1, R):
            pltpu.make_async_remote_copy(
                src_ref=src,
                dst_ref=land.at[t, me_r, p],
                send_sem=ag_s.at[t],
                recv_sem=ag_r.at[t, j - 1],
                device_id=(lax.rem(me_r + j, R), me_e),
                device_id_type=MESH,
            ).start()

    own = []
    for t in range(2):
        loads[t].wait()
        v = jnp.dot(place_t, tg_v[t], preferred_element_type=F32)
        if t == 1:
            v = slot_gate * v
        for p in range(E):
            sendb[t, p] = v[CAP * p : CAP * p + CAP].astype(BF16)
        for k in range(1, E):
            p = lax.rem(me_e + k, E)
            pltpu.make_async_remote_copy(
                src_ref=sendb.at[t, p],
                dst_ref=land.at[t, me_r, me_e],
                send_sem=a2a_s.at[t],
                recv_sem=a2a_r.at[t, k - 1],
                device_id=(me_r, p),
                device_id_type=MESH,
            ).start()
        c = pltpu.make_async_copy(sendb.at[t, me_e], land.at[t, me_r, me_e], own_sem.at[t])
        c.start()
        own.append(c)
        forward(t, sendb.at[t, me_e], me_e)

    for t in range(2):
        for k in range(1, E):
            p = lax.rem(me_e + E - k, E)
            pltpu.make_async_copy(land.at[t, me_r, p], land.at[t, me_r, p], a2a_r.at[t, k - 1]).wait()
            forward(t, land.at[t, me_r, p], p)

    def assemble(t):
        own[t].wait()
        for j in range(R):
            r = lax.rem(me_r + R - j, R)
            if j > 0:
                pltpu.make_async_copy(land.at[t, r], land.at[t, r], ag_r.at[t, j - 1]).wait()
            for p in range(E):
                xf[CAP * p : CAP * p + CAP, :] = land[t, r, p].astype(F32)
            rows_o[t, r] = xf[...].astype(BF16)

    def send_parts(t):
        for j in range(1, R):
            r = lax.rem(me_r + j, R)
            pltpu.make_async_remote_copy(
                src_ref=part.at[t, r],
                dst_ref=rs.at[t, j - 1],
                send_sem=rs_s.at[t],
                recv_sem=rs_r.at[t, j - 1],
                device_id=(r, me_e),
                device_id_type=MESH,
            ).start()

    CH = 512

    assemble(0)
    loads[2].wait()
    loads[3].wait()
    x = rows_o[0].reshape(N, D)
    gate_pre = jnp.dot(x, wg_v[...], preferred_element_type=F32)
    up_pre = jnp.dot(x, wu_v[...], preferred_element_type=F32)
    sig = jax.nn.sigmoid(gate_pre)
    active = gate_pre * sig
    hidden = (active * up_pre).astype(BF16)
    hid_o[...] = hidden
    loads[4].wait()
    for c in range(D // CH):
        cols = slice(c * CH, c * CH + CH)
        o = jnp.dot(hidden, wd_v[:, cols], preferred_element_type=F32)
        part[0, :, :, cols] = o.astype(BF16).reshape(R, S, CH)
    send_parts(0)

    assemble(1)
    g = rows_o[1].reshape(N, D)
    hg = lax.dot_general(g, wd_v[...], LAST, preferred_element_type=F32)
    gg = (hg * up_pre * sig * (1.0 + gate_pre * (1.0 - sig))).astype(BF16)
    ug = (hg * active).astype(BF16)
    gg_o[...] = gg
    ug_o[...] = ug
    for c in range(D // CH):
        cols = slice(c * CH, c * CH + CH)
        o = lax.dot_general(gg, wg_v[cols, :], LAST, preferred_element_type=F32)
        o = o + lax.dot_general(ug, wu_v[cols, :], LAST, preferred_element_type=F32)
        part[1, :, :, cols] = o.astype(BF16).reshape(R, S, CH)
    send_parts(1)

    for t in range(2):
        total = part[t, me_r].astype(F32)
        for j in range(1, R):
            pltpu.make_async_copy(rs.at[t, j - 1], rs.at[t, j - 1], rs_r.at[t, j - 1]).wait()
            total = total + rs[t, j - 1].astype(F32)
        for p in range(E):
            back[t, p] = total[CAP * p : CAP * p + CAP].astype(BF16)
        for k in range(1, E):
            p = lax.rem(me_e + k, E)
            pltpu.make_async_remote_copy(
                src_ref=back.at[t, p],
                dst_ref=ret.at[t, me_e],
                send_sem=bk_s.at[t],
                recv_sem=bk_r.at[t, k - 1],
                device_id=(me_r, p),
                device_id_type=MESH,
            ).start()
        pltpu.make_async_copy(back.at[t, me_e], ret.at[t, me_e], own_sem.at[2 + t]).start()

    for t in range(2):
        pltpu.make_async_copy(back.at[t, me_e], ret.at[t, me_e], own_sem.at[2 + t]).wait()
        for k in range(1, E):
            p = lax.rem(me_e + E - k, E)
            pltpu.make_async_copy(ret.at[t, p], ret.at[t, p], bk_r.at[t, k - 1]).wait()
        for p in range(E):
            xf[CAP * p : CAP * p + CAP, :] = ret[t, p].astype(F32)
        ret_o[t] = xf[...].astype(BF16)

    for t in range(2):
        few = pl.ds(0, E - 1)
        pltpu.make_async_copy(sendb.at[t, few], sendb.at[t, few], a2a_s.at[t]).wait()
        pltpu.make_async_copy(back.at[t, few], back.at[t, few], bk_s.at[t]).wait()
        most = pl.ds(0, R - 1)
        pltpu.make_async_copy(land.at[t, most], land.at[t, most], ag_s.at[t]).wait()
        pltpu.make_async_copy(part.at[t, most], part.at[t, most], rs_s.at[t]).wait()


def write_kernel(
    rows, grads, hid, gg, ug, ret, place, w, comb_o, tgrad_o, wg_o, wu_o, wd_o
):
    x = rows[0]
    wg_o[0] = lax.dot_general(x, gg[...], FIRST, preferred_element_type=F32).astype(BF16)
    wu_o[0] = lax.dot_general(x, ug[...], FIRST, preferred_element_type=F32).astype(BF16)
    wd_o[0] = lax.dot_general(hid[...], grads[0], FIRST, preferred_element_type=F32).astype(BF16)
    comb_o[...] = (
        jnp.dot(place[...], ret[0], preferred_element_type=F32) * w[...]
    ).astype(BF16)
    tgrad_o[...] = jnp.dot(place[...], ret[1], preferred_element_type=F32).astype(BF16)


def on_device(R, E, tokens, routes, gates, gate_weight, up_weight, down_weight, grad_out):
    T, D = tokens.shape
    U = gate_weight.shape[2]
    S = E * CAP
    N = R * S
    vm = pl.BlockSpec(memory_space=pltpu.VMEM)
    hb = pl.BlockSpec(memory_space=pl.ANY)
    dma = pltpu.SemaphoreType.DMA
    sds = jax.ShapeDtypeStruct
    rows, hid, gg, ug, ret, place, w = pl.pallas_call(
        functools.partial(exchange_kernel, R, E),
        out_shape=(
            sds((2, R, S, D), BF16),
            sds((N, U), BF16),
            sds((N, U), BF16),
            sds((N, U), BF16),
            sds((2, S, D), BF16),
            sds((T, S), BF16),
            sds((T, 1), F32),
        ),
        in_specs=[vm, vm, hb, hb, hb, hb, hb],
        out_specs=[vm] * 7,
        scratch_shapes=[
            pltpu.VMEM((2, T, D), BF16),
            pltpu.VMEM((D, U), BF16),
            pltpu.VMEM((D, U), BF16),
            pltpu.VMEM((U, D), BF16),
            pltpu.VMEM((2, E, CAP, D), BF16),
            pltpu.VMEM((2, R, E, CAP, D), BF16),
            pltpu.VMEM((S, D), F32),
            pltpu.VMEM((2, R, S, D), BF16),
            pltpu.VMEM((2, R - 1, S, D), BF16),
            pltpu.VMEM((2, E, CAP, D), BF16),
            pltpu.VMEM((2, E, CAP, D), BF16),
            dma((5,)),
            dma((4,)),
            dma((2,)),
            dma((2, E - 1)),
            dma((2,)),
            dma((2, R - 1)),
            dma((2,)),
            dma((2, R - 1)),
            dma((2,)),
            dma((2, E - 1)),
        ],
        compiler_params=pltpu.CompilerParams(
            collective_id=0, has_side_effects=True, vmem_limit_bytes=60 * 1024 * 1024
        ),
        name="exchange",
    )(routes, gates, tokens, grad_out, gate_weight, up_weight, down_weight)
    rows = rows.reshape(2, N, D)
    CH = 512
    full = lambda *shape: pl.BlockSpec(shape, lambda i: (0,) * len(shape))
    return pl.pallas_call(
        write_kernel,
        grid=(D // CH,),
        out_shape=(
            sds((T, D), BF16),
            sds((T, D), BF16),
            sds((1, D, U), BF16),
            sds((1, D, U), BF16),
            sds((1, U, D), BF16),
        ),
        in_specs=[
            pl.BlockSpec((1, N, CH), lambda i: (0, 0, i)),
            pl.BlockSpec((1, N, CH), lambda i: (1, 0, i)),
            full(N, U),
            full(N, U),
            full(N, U),
            pl.BlockSpec((2, S, CH), lambda i: (0, 0, i)),
            full(T, S),
            full(T, 1),
        ],
        out_specs=(
            pl.BlockSpec((T, CH), lambda i: (0, i)),
            pl.BlockSpec((T, CH), lambda i: (0, i)),
            pl.BlockSpec((1, CH, U), lambda i: (0, i, 0)),
            pl.BlockSpec((1, CH, U), lambda i: (0, i, 0)),
            pl.BlockSpec((1, U, CH), lambda i: (0, 0, i)),
        ),
        name="weight_grads",
    )(rows, rows, hid, gg, ug, ret, place, w)


def solution(mesh):
    placed = (
        P(("rep", "exp"), None),
        P(("rep", "exp"), None),
        P(("rep", "exp"), None),
        P("exp", None, "rep"),
        P("exp", None, "rep"),
        P("exp", "rep", None),
        P(("rep", "exp"), None),
    )
    return jax.shard_map(
        functools.partial(on_device, mesh.shape["rep"], mesh.shape["exp"]),
        mesh=mesh,
        in_specs=placed,
        out_specs=(
            P(("rep", "exp"), None),
            P(("rep", "exp"), None),
            P("exp", None, "rep"),
            P("exp", None, "rep"),
            P("exp", "rep", None),
        ),
        check_vma=False,
    )
```

time: 135 us -> 48.2 us (0.36)
  Pallas kernels: 0 us -> 44.1 us
  waiting for transfers between devices: 37.8 us -> 0 us
  matrix products: 26.5 us -> 0 us
  blocking collectives: 20.2 us -> 0 us
  starting transfers between devices: 19 us -> 0 us
  between operations: 14.2 us -> 0.64 us
  local copies, waits for them, and re-layouts: 14.5 us -> 2.83 us
  other arithmetic: 1.97 us -> 0 us
    pallas_call x0 -> x2, Pallas kernels: none -> 44.1 us  [the longest x1 35.8 us: on_device(): pl.pallas_call(functools.partial(exchange_kernel, R, E), out_shape=(sds((...]
    reduce_scatter x2 -> x0, waiting for transfers between devices: 28.1 us -> none  [reduce_rows(): lax.psum_scatter(term_fn(jnp.int32(0), row_count * lax.axis_size('rep'))....]
    dot_general x10 -> x0, matrix products: 26.5 us -> none  [the longest x1 5.49 us: input_term(): jnp.einsum('sgcu,du->gscd', grid, joined, preferred_element_type=jnp.floa...]
    all_gather x2 -> x0, blocking collectives: 20.2 us -> none  [deliver(): arrived = lax.all_gather(landed, 'rep', axis=1, tiled=True)]
    all_to_all x4 -> x0, starting transfers between devices: 18.9 us -> none  [the longest x2 9.72 us: deliver(): lax.all_to_all(slot_rows, 'exp', split_axis=0, concat_axis=0, tiled=True)]
    all_to_all x4 -> x0, waiting for transfers between devices: 9.58 us -> none  [the longest x2 5.16 us: send_back(): lax.all_to_all(slot_rows, 'exp', split_axis=0, concat_axis=0, tiled=True)]
    broadcast_in_dim x3 -> x0, local copies, waits for them, and re-layouts: 6.68 us -> none  [the longest x1 6.67 us: on_device(): up_weight_grad = joined_grad[:, units:].astype(jnp.bfloat16)[None]]
    reshape x5 -> x0, local copies, waits for them, and re-layouts: 4.63 us -> none  [the longest x1 1.59 us: on_device(): mine_out.reshape(experts_here, CAP, features)]
  transfers between devices with their start and end apart: 6 -> 0, of which waited for: 4 -> 0; matrix products, arithmetic and copies ran while one was open for 19% -> 0% of each run, Pallas kernels for 0% -> 0%
where the time goes in v1:
time: 48.2 us; the launch traced here: 47.6 us
  Pallas kernels  44.1 us (91%)
  local copies, waits for them, and re-layouts  2.83 us (6%)
  between operations  0.64 us (1%)
    pallas_call x1, Pallas kernels, on_device(): pl.pallas_call(functools.partial(exchange_kernel, R, E), out_shape=(sds((...  35.8 us
    pallas_call x1, Pallas kernels, on_device(): pl.pallas_call(write_kernel, grid=(D // CH,), out_shape=(sds((T, D), BF16...  8.25 us
    unnamed x2, local copies, waits for them, and re-layouts  2.83 us

profile of v1, /device:TPU:0, one launch (start us, length us, event | category | flops | bytes accessed | tf_op | source)
XLA Modules:
  0.0 47.6 jit_solution(7826778002818346560)
XLA Ops:
  0.6 1.4 %copy.12.routes = s32[128,8]{1,0:T(8,128)} copy(s32[128,8]{0,1:T(8,128)} %param.8) | data formatting | bytes 8192 | tf_op args[1]
  2.0 1.4 %copy.13.gates = f32[128,8]{1,0:T(8,128)} copy(f32[128,8]{0,1:T(8,128)} %param.9) | data formatting | bytes 8192 | tf_op args[2]
  3.5 35.8 %exchange.1 = (bf16[2,4,16,3584]{3,2,1,0:T(8,128)(2,1)}, bf16[64,512]{1,0:T(8,128)(2,1)}, bf16[64,512]{1,0:T(8,128)(2,1)}, bf16[64,512]{1,0:T(8,128)(2,1)}, bf16...) custom-call(s32[128,8]{1,0:T(8,128)} %copy.12.routes, f32[128,8]{1,0:T(8,128)} %copy.13.gates, ...), custom_call_target="tpu_custom_call" | custom-call | tf_op jit(solution)/shard_map/exchange/pallas_call | solution.py:256
  39.3 8.2 %weight_grads.1 = (bf16[128,3584]{1,0:T(8,128)(2,1)}, bf16[128,3584]{1,0:T(8,128)(2,1)}, bf16[1,3584,512]{2,1,0:T(8,128)(2,1)}, bf16[1,3584,512]{2,1,0:T(8,128)(2,1)}, bf16[1,512,3584]{2,1,0:T(8,128)(2,1)}) custom-call(bf16[2,64,3584]{2,1,0:T(8,128)(2,1)} %bitcast.1, bf16[2,64,3584]{2,1,0:T(8,128)(2,1)} %bitcast.2, bf16[64,512]{1,0:T(8,128)(2,1)} %get-tuple-element.13.hid, ...), custom_call_target="tpu_custom_call" | custom-call | tf_op jit(solution)/shard_map/weight_grads/pallas_call | solution.py:300

commit v2 on v1

--- a/solution.py
+++ b/solution.py
@@ -67,8 +67,8 @@
         pltpu.make_async_copy(wu_h.at[0], wu_v, in_sem.at[3]),
         pltpu.make_async_copy(wd_h.at[0], wd_v, in_sem.at[4]),
     ]
-    for c in loads:
-        c.start()
+    loads[0].start()
+    loads[1].start()
     barrier = pltpu.get_barrier_semaphore()
     for k in range(1, E):
         pl.semaphore_signal(
@@ -80,22 +80,20 @@
         )
 
     live = routes[...] < E
-    eid = jnp.sum(jnp.where(live, routes[...].astype(F32) + 1.0, 0.0), axis=1, keepdims=True) - 1.0
-    w = jnp.sum(jnp.where(live, gates[...], 0.0), axis=1, keepdims=True)
+    eid = jnp.sum(jnp.where(live, routes[...].astype(F32) + 1.0, 0.0), axis=0, keepdims=True) - 1.0
+    w = jnp.sum(jnp.where(live, gates[...], 0.0), axis=0, keepdims=True)
     lanes = lax.broadcasted_iota(jnp.int32, (T, T), 1)
     subs = lax.broadcasted_iota(jnp.int32, (T, T), 0)
-    picked = jnp.where(eid == lanes.astype(F32), 1.0, 0.0)
-    lower = jnp.where(lanes < subs, 1.0, 0.0).astype(BF16)
-    before = jnp.dot(lower, picked.astype(BF16), preferred_element_type=F32)
-    pos = jnp.sum(picked * before, axis=1, keepdims=True)
+    picked = jnp.where(eid == subs[:S].astype(F32), 1.0, 0.0)
+    upper = jnp.where(subs < lanes, 1.0, 0.0).astype(BF16)
+    before = jnp.dot(picked.astype(BF16), upper, preferred_element_type=F32)
+    pos = jnp.sum(picked * before, axis=0, keepdims=True)
     slot = jnp.where(eid >= 0.0, eid * CAP + pos, -1.0)
-    place_o[...] = jnp.where(slot == lanes[:, :S].astype(F32), 1.0, 0.0).astype(BF16)
-    w_o[...] = w
-    slot_t = jnp.transpose(jnp.broadcast_to(slot, (T, T)))[:S]
-    w_t = jnp.transpose(jnp.broadcast_to(w, (T, T)))[:S]
-    placed_t = slot_t == subs[:S].astype(F32)
+    placed_t = slot == subs[:S].astype(F32)
     place_t = jnp.where(placed_t, 1.0, 0.0).astype(BF16)
-    slot_gate = jnp.sum(jnp.where(placed_t, w_t, 0.0), axis=1, keepdims=True)
+    slot_gate = jnp.sum(jnp.where(placed_t, w, 0.0), axis=1, keepdims=True)
+    place_o[...] = place_t
+    w_o[...] = jnp.transpose(jnp.broadcast_to(w, (T, T)))[:, :1]
 
     pl.semaphore_wait(barrier, E + R - 2)
 
@@ -133,6 +131,8 @@
         own.append(c)
         forward(t, sendb.at[t, me_e], me_e)
 
+    for c in loads[2:]:
+        c.start()
     for t in range(2):
         for k in range(1, E):
             p = lax.rem(me_e + E - k, E)
@@ -239,9 +239,9 @@
     wu_o[0] = lax.dot_general(x, ug[...], FIRST, preferred_element_type=F32).astype(BF16)
     wd_o[0] = lax.dot_general(hid[...], grads[0], FIRST, preferred_element_type=F32).astype(BF16)
     comb_o[...] = (
-        jnp.dot(place[...], ret[0], preferred_element_type=F32) * w[...]
+        lax.dot_general(place[...], ret[0], FIRST, preferred_element_type=F32) * w[...]
     ).astype(BF16)
-    tgrad_o[...] = jnp.dot(place[...], ret[1], preferred_element_type=F32).astype(BF16)
+    tgrad_o[...] = lax.dot_general(place[...], ret[1], FIRST, preferred_element_type=F32).astype(BF16)
 
 
 def on_device(R, E, tokens, routes, gates, gate_weight, up_weight, down_weight, grad_out):
@@ -261,7 +261,7 @@
             sds((N, U), BF16),
             sds((N, U), BF16),
             sds((2, S, D), BF16),
-            sds((T, S), BF16),
+            sds((S, T), BF16),
             sds((T, 1), F32),
         ),
         in_specs=[vm, vm, hb, hb, hb, hb, hb],
@@ -293,9 +293,9 @@
             collective_id=0, has_side_effects=True, vmem_limit_bytes=60 * 1024 * 1024
         ),
         name="exchange",
-    )(routes, gates, tokens, grad_out, gate_weight, up_weight, down_weight)
+    )(routes.T, gates.T, tokens, grad_out, gate_weight, up_weight, down_weight)
     rows = rows.reshape(2, N, D)
-    CH = 512
+    CH = D // 4
     full = lambda *shape: pl.BlockSpec(shape, lambda i: (0,) * len(shape))
     return pl.pallas_call(
         write_kernel,
@@ -314,7 +314,7 @@
             full(N, U),
             full(N, U),
             pl.BlockSpec((2, S, CH), lambda i: (0, 0, i)),
-            full(T, S),
+            full(S, T),
             full(T, 1),
         ],
         out_specs=(

time: 48.2 us -> 43.7 us (0.907)
  local copies, waits for them, and re-layouts: 2.83 us -> 0 us
  Pallas kernels: 44.1 us -> 42.8 us
    unnamed x2 -> x0, local copies, waits for them, and re-layouts: 2.83 us -> none
    pallas_call x1, Pallas kernels: 8.25 us -> 7.15 us  [on_device(): pl.pallas_call(write_kernel, grid=(D // CH,), out_shape=(sds((T, D), BF16...]
where the time goes in v2:
time: 43.7 us; the launch traced here: 43.5 us
  Pallas kernels  42.8 us (98%)
  between operations  0.64 us (1%)
    pallas_call x1, Pallas kernels, on_device(): pl.pallas_call(functools.partial(exchange_kernel, R, E), out_shape=(sds((...  35.7 us
    pallas_call x1, Pallas kernels, on_device(): pl.pallas_call(write_kernel, grid=(D // CH,), out_shape=(sds((T, D), BF16...  7.15 us

profile of v2, /device:TPU:0, one launch (start us, length us, event | category | flops | bytes accessed | tf_op | source)
XLA Modules:
  0.0 43.5 jit_solution(10873500240181553861)
XLA Ops:
  0.6 35.7 %exchange.1 = (bf16[2,4,16,3584]{3,2,1,0:T(8,128)(2,1)}, bf16[64,512]{1,0:T(8,128)(2,1)}, bf16[64,512]{1,0:T(8,128)(2,1)}, bf16[64,512]{1,0:T(8,128)(2,1)}, bf16...) custom-call(s32[8,128]{1,0:T(8,128)} %bitcast.5, f32[8,128]{1,0:T(8,128)} %bitcast.6, ...), custom_call_target="tpu_custom_call" | custom-call | tf_op jit(solution)/shard_map/exchange/pallas_call | solution.py:256
  36.3 7.1 %weight_grads.1 = (bf16[128,3584]{1,0:T(8,128)(2,1)}, bf16[128,3584]{1,0:T(8,128)(2,1)}, bf16[1,3584,512]{2,1,0:T(8,128)(2,1)}, bf16[1,3584,512]{2,1,0:T(8,128)(2,1)}, bf16[1,512,3584]{2,1,0:T(8,128)(2,1)}) custom-call(bf16[2,64,3584]{2,1,0:T(8,128)(2,1)} %bitcast.3, bf16[2,64,3584]{2,1,0:T(8,128)(2,1)} %bitcast.4, bf16[64,512]{1,0:T(8,128)(2,1)} %get-tuple-element.13.hid, ...), custom_call_target="tpu_custom_call" | custom-call | tf_op jit(solution)/shard_map/weight_grads/pallas_call | solution.py:300
